TPU v7x, 256 devices: a whole 4x4x8 slice. The times are simulated.
256 devices in a mesh: seq: 64 (over y, z, x_lo), head: 4 (over x_hi, core).
Axes of the slice: x: 4 (x_hi: 2, x_lo: 2; x = x_hi * 2 + x_lo), y: 4, z: 8, core: 2. Of those that a mesh axis runs over, the one named last changes fastest.
Arguments:
- inputs: bfloat16 [32768, 5376], P('seq'), may hold values from -6 to 6
- queries: bfloat16 [32768, 16, 128], P('seq', 'head'), may hold values from -24 to 24
- out_grad: bfloat16 [32768, 16, 128], P('seq', 'head'), may hold values from -6 to 6
- segment_ids: int32 [32768], P('seq'), may hold values from 0 to 63, never falling along the last dimension, each value on 1 to 2048 neighbouring positions
- k_weight: bfloat16 [5376, 1024], P('seq', 'head'), may hold values from -0.078125 to 0.078125
- v_weight: bfloat16 [5376, 1024], P('seq', 'head'), may hold values from -0.078125 to 0.078125
- k_gain: float32 [128], replicated, may hold values from 0.1 to 1.9
Outputs:
- inputs_grad: bfloat16 [32768, 5376], P('seq', 'head')
- query_grad: bfloat16 [32768, 16, 128], P('seq', 'head')
- k_weight_grad: float32 [5376, 1024], P('seq', 'head')
- v_weight_grad: float32 [5376, 1024], P('seq', 'head')
Inputs may be any that keep to these rules, and one draw needn't show every extreme that they name: `segment_ids`: tokens of one packed document share an id; ids never fall along the row; a document holds at most 2048 tokens.
All inputs are finite; a program needn't handle non-finite values.
Results may differ from a plain program's by a relative error of at most 0.01065.
The roundings to bfloat16 on the way count: a program that leaves them out, or rounds other values in their place, can miss the bound.
Values may be sent and summed in bfloat16 or wider, within the bound.
No kernel may reach another device: no remote copies, remote signals or barrier semaphores. Data moves between devices by JAX's collectives and lax.ppermute only.
A program may use at most 128 MiB of HBM per device.

v0:
```python
import jax
import jax.numpy as jnp
from jax import lax
from jax.sharding import PartitionSpec as P

WIN = 1024
TOK_DEV = 512
score_scale = 168.0 ** (-0.5)


def shifted(block, axis, distance):
    devices = range(lax.axis_size(axis))
    route = [(i - distance, i) for i in devices if i - distance in devices]
    return lax.ppermute(block, axis, route)


def make_allowed(query_pos, query_seg, key_pos, key_seg):
    distance = query_pos[:, None] - key_pos[None, :]
    return (
        (distance >= 0)
        & (distance < WIN)
        & (query_seg[:, None] == key_seg[None, :])
        & (key_pos[None, :] >= 0)
    )


def score_block(query_view, key_block, allowed):
    scores = (
        jnp.einsum("qkgd,ckd->kgqc", query_view, key_block, preferred_element_type=jnp.float32)
        * score_scale
    )
    return jnp.where(allowed[None, None], scores, -1e30)


def score_grads(probs, grad_view, value_block, delta):
    prob_grad = jnp.einsum(
        "qkgd,ckd->kgqc", grad_view, value_block, preferred_element_type=jnp.float32
    )
    return (probs * (prob_grad - delta[..., None])).astype(jnp.bfloat16)


def key_grads(probs_low, score_grad, query_view, grad_view):
    key_grad = (
        jnp.einsum("kgqc,qkgd->ckd", score_grad, query_view, preferred_element_type=jnp.float32)
        * score_scale
    )
    value_grad = jnp.einsum(
        "kgqc,qkgd->ckd", probs_low, grad_view, preferred_element_type=jnp.float32
    )
    return (key_grad, value_grad)


def per_device(inputs, queries, out_grad, segment_ids, k_weight, v_weight, k_gain):
    tok_rows = inputs.shape[0]
    head_dim = queries.shape[2]
    kv_local = k_weight.shape[1] // head_dim
    group_size = queries.shape[1] // kv_local
    seq_index = lax.axis_index("seq")
    reach_count = WIN // TOK_DEV
    row_base = seq_index * tok_rows
    local_pos = row_base + jnp.arange(tok_rows, dtype=jnp.int32)
    k_full, v_full = (
        lax.all_gather(k_weight, "seq", axis=0, tiled=True),
        lax.all_gather(v_weight, "seq", axis=0, tiled=True),
    )
    k_raw = jnp.dot(inputs, k_full, preferred_element_type=jnp.float32)
    v_raw = jnp.dot(inputs, v_full, preferred_element_type=jnp.float32)
    k_raw = k_raw.reshape(tok_rows, kv_local, head_dim)
    k_inv = lax.rsqrt(jnp.mean(k_raw * k_raw, axis=-1, keepdims=True) + 1e-06)
    k_normed = k_raw * k_inv
    keys_own = (k_normed * k_gain).astype(jnp.bfloat16)
    values_own = v_raw.astype(jnp.bfloat16).reshape(tok_rows, kv_local, head_dim)
    key_list = [keys_own]
    value_list = [values_own]
    seg_list = [segment_ids]
    for offset in range(1, reach_count + 1):
        prior_keys, prior_values, prior_seg = shifted(
            (keys_own, values_own, segment_ids), "seq", offset
        )
        key_list = [prior_keys] + key_list
        value_list = [prior_values] + value_list
        seg_list = [prior_seg] + seg_list
    key_block = jnp.concatenate(key_list, 0)
    value_block = jnp.concatenate(value_list, 0)
    key_seg = jnp.concatenate(seg_list, 0)
    key_pos = (
        row_base
        - reach_count * tok_rows
        + jnp.arange((reach_count + 1) * tok_rows, dtype=jnp.int32)
    )
    query_view = queries.reshape(tok_rows, kv_local, group_size, head_dim)
    grad_view = out_grad.reshape(tok_rows, kv_local, group_size, head_dim)
    allowed = make_allowed(local_pos, segment_ids, key_pos, key_seg)
    scores = score_block(query_view, key_block, allowed)
    row_peak = jnp.max(scores, axis=-1, keepdims=True)
    log_total = row_peak[..., 0] + jnp.log(jnp.sum(jnp.exp(scores - row_peak), axis=-1))
    probs = jnp.exp(scores - log_total[..., None])
    probs_low = probs.astype(jnp.bfloat16)
    attn_out = jnp.einsum(
        "kgqc,ckd->qkgd", probs_low, value_block, preferred_element_type=jnp.float32
    )
    delta = jnp.transpose(jnp.sum(grad_view.astype(jnp.float32) * attn_out, axis=-1), (1, 2, 0))
    score_grad = score_grads(probs, grad_view, value_block, delta)
    query_grad = (
        jnp.einsum("kgqc,ckd->qkgd", score_grad, key_block, preferred_element_type=jnp.float32)
        * score_scale
    )
    key_all, value_all = key_grads(probs_low, score_grad, query_view, grad_view)
    own_lower = reach_count * tok_rows
    key_grad = key_all[own_lower:]
    value_grad = value_all[own_lower:]
    for offset in range(1, reach_count + 1):
        lower = (reach_count - offset) * tok_rows
        back_keys, back_values = shifted(
            (key_all[lower : lower + tok_rows], value_all[lower : lower + tok_rows]), "seq", -offset
        )
        key_grad = key_grad + back_keys
        value_grad = value_grad + back_values
    normed_grad = key_grad * k_gain
    raw_grad = (
        normed_grad - k_normed * jnp.mean(normed_grad * k_normed, axis=-1, keepdims=True)
    ) * k_inv
    raw_low = raw_grad.astype(jnp.bfloat16).reshape(tok_rows, kv_local * head_dim)
    value_low = value_grad.astype(jnp.bfloat16).reshape(tok_rows, kv_local * head_dim)
    input_term = jnp.dot(raw_low, k_full.T, preferred_element_type=jnp.float32)
    input_term = input_term + jnp.dot(value_low, v_full.T, preferred_element_type=jnp.float32)
    inputs_grad = lax.psum_scatter(
        input_term.astype(jnp.bfloat16), "head", scatter_dimension=1, tiled=True
    )
    both_grads = jnp.concatenate([raw_low, value_low], 1)
    split_at = kv_local * head_dim
    weight_rows_grad = lax.psum_scatter(
        lax.dot_general(
            inputs, both_grads, (((0,), (0,)), ((), ())), preferred_element_type=jnp.float32
        ),
        "seq",
        scatter_dimension=0,
        tiled=True,
    )
    return (
        inputs_grad,
        query_grad.astype(jnp.bfloat16).reshape(tok_rows, kv_local * group_size, head_dim),
        weight_rows_grad[:, :split_at],
        weight_rows_grad[:, split_at:],
    )


def solution(mesh):
    in_specs = (
        P("seq", None),
        P("seq", "head", None),
        P("seq", "head", None),
        P("seq"),
        P("seq", "head"),
        P("seq", "head"),
        P(),
    )
    out_specs = (P("seq", "head"), P("seq", "head", None), P("seq", "head"), P("seq", "head"))
    return jax.shard_map(
        per_device, mesh=mesh, in_specs=in_specs, out_specs=out_specs, check_vma=False
    )
```

profile of v0, /device:TPU:1, one launch (start us, length us, event | category | flops | bytes accessed | tf_op | source)
XLA Modules:
  0.0 1416.5 jit_solution(10435968799041910594)
XLA Ops:
  7.2 0.0 all-gather.5.cloned.1.call-start
  7.2 0.7 all-gather.5.cloned.1.call-update
  7.9 0.0 all-gather.7.cloned.1.call-start
  7.9 0.7 all-gather.7.cloned.1.call-update
  8.6 0.0 all-reduce.3.cloned.1.call-start
  8.7 4.4 collective-permute-start
  13.1 3.1 collective-permute-start.1
  16.2 2.0 copy.58
  18.3 2.1 copy.79
  20.4 0.7 pad_add_fusion
  21.1 3.2 fusion.6
  24.3 243.2 %all-gather.5.cloned.1.call-done = bf16[64,84,256]{2,1,0:T(8,128)(2,1)} async-done(((bf16[1,84,256]{2,1,0:T(8,128)(2,1)}), bf16[64,84,256]{2,1,0:T(8,128)(2,1)}) %all-gather.5.cloned.1.call-update) | async-done | bytes 2752528 | tf_op jit(solution)/shard_map/all_gather | solution.py:63
  267.5 3.6 reshape.143
  271.1 0.0 copy-start.7
  271.1 6.0 multiply_reduce_fusion.1
  277.1 1.2 copy.48
  278.3 0.9 multiply_convert_fusion.1
  279.2 2.0 collective-permute-start.3
  281.2 2.7 collective-permute-start.2
  283.9 284.6 %all-gather.7.cloned.1.call-done = bf16[64,84,256]{2,1,0:T(8,128)(2,1)} async-done(((bf16[1,84,256]{2,1,0:T(8,128)(2,1)}), bf16[64,84,256]{2,1,0:T(8,128)(2,1)}) %all-gather.7.cloned.1.call-update) | async-done | bytes 2752528 | tf_op jit(solution)/shard_map/all_gather | solution.py:64
  568.5 3.6 reshape.145
  572.1 4.9 convolution_convert_fusion
  577.0 1.1 copy.50
  578.1 0.0 copy-start.2
  578.1 1.4 collective-permute-start.5
  579.5 2.6 collective-permute-start.4
  582.2 0.0 collective-permute-done.3
  582.2 0.0 collective-permute-done.2
  582.2 4.2 fusion.3
  586.4 2.8 exponential_reduce_fusion
  589.2 0.0 copy-start.8
  589.2 0.0 collective-permute-done.4
  589.3 3.7 fusion.11
  593.0 8.2 fusion.1
  601.2 4.8 fusion.8
  606.0 0.1 fusion.30
  606.0 1.3 collective-permute-start.6
  607.3 1.3 collective-permute-start.7
  608.7 6.6 convolution_bitcast_fusion.1
  615.2 1.2 fusion.29
  616.4 1.3 collective-permute-start.8
  617.7 1.5 collective-permute-start.9
  619.3 2.6 collective-permute-done.7
  621.9 0.4 multiply_reduce_fusion
  622.3 0.3 multiply_convert_fusion
  622.6 0.1 copy.60
  622.8 4.5 collective-permute-done.8
  627.3 6.8 collective-permute-done.9
  634.1 1.5 fusion.13
  635.6 8.5 convolution_bitcast_fusion
  644.0 0.0 all-reduce.3.cloned.1.call-update
  644.1 0.0 reduce-scatter.3.cloned.1.call-start
  644.1 3.4 fusion.31
  647.5 4.0 add_convert_fusion
  651.4 0.0 reduce-scatter.3.cloned.1.call-update
  651.5 0.6 copy-done.10
  652.1 0.6 dynamic-slice
  653.3 4.1 fusion.10
  657.5 1.1 copy.64
  658.5 644.2 %all-reduce.3.cloned.1.call-done = f32[5376,512]{0,1:T(8,128)} async-done(((f32[5376,512]{0,1:T(8,128)}), f32[5376,512]{0,1:T(8,128)}) %all-reduce.3.cloned.1.call-update) | async-done | bytes 11010064
  1302.7 1.2 fusion.28
  1303.9 0.7 copy.66
  1304.6 0.7 copy.65
  1305.3 104.7 %reduce-scatter.3.cloned.1.call-done = bf16[512,1344]{0,1:T(8,128)(2,1)} async-done(((bf16[512,5376]{0,1:T(8,128)(2,1)}), bf16[512,1344]{0,1:T(8,128)(2,1)}) %reduce-scatter.3.cloned.1.call-update) | async-done | bytes 1376272 | tf_op jit(solution)/shard_map/reduce_scatter | solution.py:127
  (28 shorter events, 0.1 us)
Async XLA Ops:
  7.2 260.3 %all-gather.5.cloned.1.call-start = ((), (), s32[]{:S(2)}) async-start(), calls=%async_computation.2 | async-start | bytes 2928640 | tf_op jit(solution)/shard_map/all_gather | solution.py:63
  7.9 560.6 %all-gather.7.cloned.1.call-start = ((), (), s32[]{:S(2)}) async-start(), calls=%async_computation.3 | async-start | bytes 2928640 | tf_op jit(solution)/shard_map/all_gather | solution.py:64
  8.6 1294.0 %all-reduce.3.cloned.1.call-start = ((), (), s32[]{:S(2)}) async-start(), calls=%async_computation.4 | async-start | bytes 22020096
  8.7 11.7 collective-permute-start
  13.1 7.3 collective-permute-start.1
  271.0 7.2 copy-start
  271.1 7.3 copy-start.7
  279.2 302.9 %collective-permute-start.3 = (bf16[512,2,128]{2,0,1:T(8,128)(2,1)}, bf16[512,2,128]{2,0,1:T(8,128)(2,1)}, u32[]{:S(2)}, u32[]{:S(2)}) collective-permute-start(bf16[512,2,128]{2,0,1:T(8,128)(2,1)} %multiply_convert_fusion.1), channel_id=1, source_target_pairs={{0,4},{4,8},{8,12},{12,16},{16,20},{20,24},{24,28},{28,32},{32,36}... | collective-permute-start | bytes 786440 | tf_op jit(solution)/shard_map/ppermute | solution.py:14
  281.2 300.9 %collective-permute-start.2 = (bf16[512,2,128]{2,0,1:T(8,128)(2,1)}, bf16[512,2,128]{2,0,1:T(8,128)(2,1)}, u32[]{:S(2)}, u32[]{:S(2)}) collective-permute-start(bf16[512,2,128]{2,0,1:T(8,128)(2,1)} %multiply_convert_fusion.1), channel_id=1, source_target_pairs={{0,8},{4,12},{8,16},{12,20},{16,24},{20,28},{24,32},{28,36},{32,40... | collective-permute-start | bytes 786440 | tf_op jit(solution)/shard_map/ppermute | solution.py:14
  578.1 8.3 copy-start.2
  578.1 11.1 collective-permute-start.5
  579.5 9.7 collective-permute-start.4
  586.4 6.6 copy-start.1
  586.4 2.8 copy-start.5
  589.2 3.7 copy-start.8
  589.3 3.7 copy-start.9
  601.2 7.5 copy-start.3
  601.2 7.5 copy-start.6
  606.0 13.2 collective-permute-start.6
  607.3 14.5 %collective-permute-start.7 = (f32[512,2,128]{2,0,1:T(8,128)S(1)}, f32[512,2,128]{2,0,1:T(8,128)S(1)}, u32[]{:S(2)}, u32[]{:S(2)}) collective-permute-start(f32[512,2,128]{2,0,1:T(8,128)S(1)} %get-tuple-element.23), channel_id=1, source_target_pairs={{8,0},{12,4},{16,8},{20,12},{24,16},{28,20},{32,24},{36,28},{40,32... | collective-permute-start | bytes 1572872 | tf_op jit(solution)/shard_map/ppermute | solution.py:14
  615.2 7.0 copy-start.4
  616.4 10.9 collective-permute-start.8
  617.7 16.4 %collective-permute-start.9 = (f32[512,2,128]{0,2,1:T(8,128)}, f32[512,2,128]{0,2,1:T(8,128)}, u32[]{:S(2)}, u32[]{:S(2)}) collective-permute-start(f32[512,2,128]{0,2,1:T(8,128)} %get-tuple-element.21), channel_id=1, source_target_pairs={{8,0},{12,4},{16,8},{20,12},{24,16},{28,20},{32,24},{36,28},{40,32... | collective-permute-start | bytes 1572872 | tf_op jit(solution)/shard_map/ppermute | solution.py:14
  644.1 765.9 %reduce-scatter.3.cloned.1.call-start = ((), (), s32[]{:S(2)}) async-start(), calls=%async_computation.1 | async-start | bytes 6881280 | tf_op jit(solution)/shard_map/reduce_scatter | solution.py:127
  651.4 0.7 copy-start.10
Sparse Core Ops, SparseCore 0:
  9.8 257.6 all-gather.4
  269.3 299.1 all-gather.6
  644.2 658.4 all-reduce.2
  1305.9 104.0 reduce-scatter.2
where the time goes:
time: 1420 us
  waiting for transfers between devices  1290 us (91%)
  matrix products  58.2 us (4%)
  starting transfers between devices  21.7 us (2%)
  local copies, waits for them, and re-layouts  20 us (1%)
  between operations  14.8 us (1%)
    unnamed x5, waiting for transfers between devices  646 us
    all_gather x1, waiting for transfers between devices, per_device(): lax.all_gather(v_weight, 'seq', axis=0, tiled=True)  285 us
    all_gather x1, waiting for transfers between devices, per_device(): lax.all_gather(k_weight, 'seq', axis=0, tiled=True)  243 us
    reduce_scatter x1, waiting for transfers between devices, per_device(): lax.psum_scatter(input_term.astype(jnp.bfloat16), 'head', scatter_dimensi...  105 us
  transfers between devices with their start and end apart: 14, of which 7 were waited for; matrix products, arithmetic and copies ran while one was open for 4% of the time, Pallas kernels for 0%

commit v1 on v0

--- a/solution.py
+++ b/solution.py
@@ -59,9 +59,13 @@
     reach_count = WIN // TOK_DEV
     row_base = seq_index * tok_rows
     local_pos = row_base + jnp.arange(tok_rows, dtype=jnp.int32)
+    region_supply = lambda chunk, pos_dim: jnp.concatenate(
+        jax.lax.all_to_all(jnp.stack(jax.lax.axis_size("seq") * [chunk], axis=0), "seq", 0, 0),
+        axis=pos_dim,
+    )
     k_full, v_full = (
         lax.all_gather(k_weight, "seq", axis=0, tiled=True),
-        lax.all_gather(v_weight, "seq", axis=0, tiled=True),
+        region_supply(v_weight, pos_dim=0),
     )
     k_raw = jnp.dot(inputs, k_full, preferred_element_type=jnp.float32)
     v_raw = jnp.dot(inputs, v_full, preferred_element_type=jnp.float32)

time: 1420 us -> 1140 us (0.80)
  waiting for transfers between devices: 1290 us -> 1010 us
    all_gather x1 -> x0, waiting for transfers between devices: 285 us -> none  [per_device(): lax.all_gather(v_weight, 'seq', axis=0, tiled=True)]
    ppermute x10, waiting for transfers between devices: 13.9 us -> 63.3 us  [shifted(): return lax.ppermute(block, axis, route)]
    all_gather x1, waiting for transfers between devices: 243 us -> 194 us  [per_device(): lax.all_gather(k_weight, 'seq', axis=0, tiled=True)]
    unnamed x5 -> x4, waiting for transfers between devices: 646 us -> 644 us
  transfers between devices with their start and end apart: 14 -> 14, of which waited for: 7 -> 7; matrix products, arithmetic and copies ran while one was open for 4% -> 5% of each run, Pallas kernels for 0% -> 0%
where the time goes in v1:
time: 1140 us
  waiting for transfers between devices  1010 us (89%)
  matrix products  58.3 us (5%)
  starting transfers between devices  33.3 us (3%)
  local copies, waits for them, and re-layouts  21 us (2%)
  between operations  14.9 us (1%)
    unnamed x4, waiting for transfers between devices  644 us
    all_gather x1, waiting for transfers between devices, per_device(): lax.all_gather(k_weight, 'seq', axis=0, tiled=True)  194 us
    reduce_scatter x1, waiting for transfers between devices, per_device(): lax.psum_scatter(input_term.astype(jnp.bfloat16), 'head', scatter_dimensi...  105 us
    ppermute x10, waiting for transfers between devices, shifted(): return lax.ppermute(block, axis, route)  63.3 us
  transfers between devices with their start and end apart: 14, of which 7 were waited for; matrix products, arithmetic and copies ran while one was open for 5% of the time, Pallas kernels for 0%

profile of v1, /device:TPU:1, one launch (start us, length us, event | category | flops | bytes accessed | tf_op | source)
XLA Modules:
  0.0 1141.6 jit_solution(6748334286839300832)
XLA Ops:
  7.2 0.0 all-gather.3.cloned.1.call-start
  7.2 0.7 all-gather.3.cloned.1.call-update
  7.9 2.6 stack.2
  10.5 13.8 %all-to-all-start = ((bf16[64,84,256]{2,1,0:T(8,128)(2,1)}), bf16[64,84,256]{2,1,0:T(8,128)(2,1)}, u32[]{:S(2)}, u32[]{:S(2)}) async-start(bf16[64,84,256]{2,1,0:T(8,128)(2,1)} %stack.2), calls=%async_computation | async-start | bytes 5767168 | tf_op jit(solution)/shard_map/all_to_all | solution.py:63
  24.3 0.0 all-reduce.3.cloned.1.call-start
  24.4 2.9 collective-permute-start
  27.2 3.1 collective-permute-start.1
  30.4 1.5 copy.58
  31.8 1.1 copy.79
  33.0 49.3 %collective-permute-done = s32[512]{0:T(512)S(1)} collective-permute-done((s32[512]{0:T(512)S(1)}, s32[512]{0:T(512)S(1)}, u32[]{:S(2)}, u32[]{:S(2)}) %collective-permute-start) | collective-permute-done | bytes 2080 | tf_op jit(solution)/shard_map/ppermute | solution.py:14
  82.3 0.0 collective-permute-done.1
  82.3 2.5 fusion.6
  84.9 194.0 %all-gather.3.cloned.1.call-done = bf16[64,84,256]{2,1,0:T(8,128)(2,1)} async-done(((bf16[1,84,256]{2,1,0:T(8,128)(2,1)}), bf16[64,84,256]{2,1,0:T(8,128)(2,1)}) %all-gather.3.cloned.1.call-update) | async-done | bytes 2752528 | tf_op jit(solution)/shard_map/all_gather | solution.py:67
  278.9 3.6 reshape.149
  282.5 0.0 copy-start.10
  282.5 6.0 multiply_reduce_fusion.1
  288.5 1.2 copy.48
  289.8 0.9 multiply_convert_fusion.1
  290.7 2.5 collective-permute-start.3
  293.2 2.0 collective-permute-start.2
  295.2 0.0 all-to-all-done
  295.2 3.6 reshape.142
  298.7 4.9 convolution_convert_fusion
  303.6 1.1 copy.50
  304.8 0.0 copy-start.2
  304.8 2.0 collective-permute-start.5
  306.8 1.5 collective-permute-start.4
  308.3 0.0 collective-permute-done.2
  308.3 4.2 fusion.3
  312.6 2.8 exponential_reduce_fusion
  315.4 0.0 copy-start.11
  315.4 0.0 collective-permute-done.4
  315.4 3.7 fusion.11
  319.1 8.2 fusion.1
  327.4 4.8 fusion.8
  332.2 0.1 fusion.30
  332.2 1.3 collective-permute-start.6
  333.5 1.3 collective-permute-start.7
  334.9 6.6 convolution_bitcast_fusion.1
  341.4 1.2 fusion.29
  342.6 1.3 collective-permute-start.8
  343.9 1.5 collective-permute-start.9
  345.4 2.1 collective-permute-done.7
  347.5 0.4 multiply_reduce_fusion
  348.0 0.3 multiply_convert_fusion
  348.3 0.1 copy.60
  348.5 5.0 collective-permute-done.8
  353.5 6.8 collective-permute-done.9
  360.3 1.5 fusion.13
  361.8 8.5 convolution_bitcast_fusion
  370.3 0.0 all-reduce.3.cloned.1.call-update
  370.3 0.0 reduce-scatter.3.cloned.1.call-start
  370.3 3.4 fusion.31
  373.7 4.0 add_convert_fusion
  377.7 0.0 reduce-scatter.3.cloned.1.call-update
  377.7 0.6 copy-done.13
  378.4 0.6 dynamic-slice
  379.6 4.1 fusion.10
  383.7 1.1 copy.64
  384.8 642.8 %all-reduce.3.cloned.1.call-done = f32[5376,512]{0,1:T(8,128)} async-done(((f32[5376,512]{0,1:T(8,128)}), f32[5376,512]{0,1:T(8,128)}) %all-reduce.3.cloned.1.call-update) | async-done | bytes 11010064
  1027.6 1.2 fusion.28
  1028.8 0.7 copy.66
  1029.5 0.7 copy.65
  1030.2 104.8 %reduce-scatter.3.cloned.1.call-done = bf16[512,1344]{0,1:T(8,128)(2,1)} async-done(((bf16[512,5376]{0,1:T(8,128)(2,1)}), bf16[512,1344]{0,1:T(8,128)(2,1)}) %reduce-scatter.3.cloned.1.call-update) | async-done | bytes 1376272 | tf_op jit(solution)/shard_map/reduce_scatter | solution.py:131
  (34 shorter events, 0.1 us)
Async XLA Ops:
  7.2 17.2 %copy-start.9 = (s32[512]{0:T(512)S(1)}, s32[512]{0:T(512)}, u32[]{:S(2)}) copy-start(s32[512]{0:T(512)} %param.10) | copy-start | bytes 6148
  7.2 23.2 %copy-start.5 = (bf16[512,4,128]{2,1,0:T(4,128)(2,1)S(1)}, bf16[512,4,128]{2,1,0:T(4,128)(2,1)}, u32[]{:S(2)}) copy-start(bf16[512,4,128]{2,1,0:T(4,128)(2,1)} %param.8) | copy-start | bytes 1572868
  7.2 24.7 %copy-start.6 = (bf16[512,4,128]{2,1,0:T(4,128)(2,1)S(1)}, bf16[512,4,128]{2,1,0:T(4,128)(2,1)}, u32[]{:S(2)}) copy-start(bf16[512,4,128]{2,1,0:T(4,128)(2,1)} %param.9) | copy-start | bytes 1572868
  7.2 271.7 %all-gather.3.cloned.1.call-start = ((), (), s32[]{:S(2)}) async-start(), calls=%async_computation.3 | async-start | bytes 2928640 | tf_op jit(solution)/shard_map/all_gather | solution.py:67
  10.5 284.7 %all-to-all-start = ((bf16[64,84,256]{2,1,0:T(8,128)(2,1)}), bf16[64,84,256]{2,1,0:T(8,128)(2,1)}, u32[]{:S(2)}, u32[]{:S(2)}) async-start(bf16[64,84,256]{2,1,0:T(8,128)(2,1)} %stack.2), calls=%async_computation | async-start | bytes 5767168 | tf_op jit(solution)/shard_map/all_to_all | solution.py:63
  24.3 1003.3 %all-reduce.3.cloned.1.call-start = ((), (), s32[]{:S(2)}) async-start(), calls=%async_computation.4 | async-start | bytes 22020096
  24.4 58.0 %collective-permute-start = (s32[512]{0:T(512)S(1)}, s32[512]{0:T(512)S(1)}, u32[]{:S(2)}, u32[]{:S(2)}) collective-permute-start(s32[512]{0:T(512)S(1)} %copy-done.9), channel_id=1, source_target_pairs={{0,8},{4,12},{8,16},{12,20},{16,24},{20,28},{24,32},{28,36},{32,40... | collective-permute-start | bytes 6152 | tf_op jit(solution)/shard_map/ppermute | solution.py:14
  27.2 55.1 %collective-permute-start.1 = (s32[512]{0:T(512)S(1)}, s32[512]{0:T(512)S(1)}, u32[]{:S(2)}, u32[]{:S(2)}) collective-permute-start(s32[512]{0:T(512)S(1)} %copy-done.9), channel_id=1, source_target_pairs={{0,4},{4,8},{8,12},{12,16},{16,20},{20,24},{24,28},{28,32},{32,36}... | collective-permute-start | bytes 6152 | tf_op jit(solution)/shard_map/ppermute | solution.py:14
  282.5 7.2 copy-start
  282.5 7.3 copy-start.10
  290.7 17.7 %collective-permute-start.3 = (bf16[512,2,128]{2,0,1:T(8,128)(2,1)}, bf16[512,2,128]{2,0,1:T(8,128)(2,1)}, u32[]{:S(2)}, u32[]{:S(2)}) collective-permute-start(bf16[512,2,128]{2,0,1:T(8,128)(2,1)} %multiply_convert_fusion.1), channel_id=1, source_target_pairs={{0,4},{4,8},{8,12},{12,16},{16,20},{20,24},{24,28},{28,32},{32,36}... | collective-permute-start | bytes 786440 | tf_op jit(solution)/shard_map/ppermute | solution.py:14
  293.2 15.2 %collective-permute-start.2 = (bf16[512,2,128]{2,0,1:T(8,128)(2,1)}, bf16[512,2,128]{2,0,1:T(8,128)(2,1)}, u32[]{:S(2)}, u32[]{:S(2)}) collective-permute-start(bf16[512,2,128]{2,0,1:T(8,128)(2,1)} %multiply_convert_fusion.1), channel_id=1, source_target_pairs={{0,8},{4,12},{8,16},{12,20},{16,24},{20,28},{24,32},{28,36},{32,40... | collective-permute-start | bytes 786440 | tf_op jit(solution)/shard_map/ppermute | solution.py:14
  304.8 7.8 copy-start.2
  304.8 10.6 collective-permute-start.5
  306.8 8.6 collective-permute-start.4
  312.6 6.6 copy-start.1
  312.6 2.8 copy-start.7
  315.4 3.7 copy-start.11
  315.4 3.7 copy-start.12
  327.4 7.5 copy-start.3
  327.4 7.5 copy-start.8
  332.2 13.2 %collective-permute-start.6 = (f32[512,2,128]{2,0,1:T(8,128)S(1)}, f32[512,2,128]{2,0,1:T(8,128)S(1)}, u32[]{:S(2)}, u32[]{:S(2)}) collective-permute-start(f32[512,2,128]{2,0,1:T(8,128)S(1)} %get-tuple-element.22), channel_id=1, source_target_pairs={{4,0},{8,4},{12,8},{16,12},{20,16},{24,20},{28,24},{32,28},{36,32}... | collective-permute-start | bytes 1572872 | tf_op jit(solution)/shard_map/ppermute | solution.py:14
  333.5 14.0 %collective-permute-start.7 = (f32[512,2,128]{2,0,1:T(8,128)S(1)}, f32[512,2,128]{2,0,1:T(8,128)S(1)}, u32[]{:S(2)}, u32[]{:S(2)}) collective-permute-start(f32[512,2,128]{2,0,1:T(8,128)S(1)} %get-tuple-element.23), channel_id=1, source_target_pairs={{8,0},{12,4},{16,8},{20,12},{24,16},{28,20},{32,24},{36,28},{40,32... | collective-permute-start | bytes 1572872 | tf_op jit(solution)/shard_map/ppermute | solution.py:14
  341.4 6.5 copy-start.4
  342.6 10.9 collective-permute-start.8
  343.9 16.4 %collective-permute-start.9 = (f32[512,2,128]{0,2,1:T(8,128)}, f32[512,2,128]{0,2,1:T(8,128)}, u32[]{:S(2)}, u32[]{:S(2)}) collective-permute-start(f32[512,2,128]{0,2,1:T(8,128)} %get-tuple-element.21), channel_id=1, source_target_pairs={{8,0},{12,4},{16,8},{20,12},{24,16},{28,20},{32,24},{36,28},{40,32... | collective-permute-start | bytes 1572872 | tf_op jit(solution)/shard_map/ppermute | solution.py:14
  370.3 764.8 %reduce-scatter.3.cloned.1.call-start = ((), (), s32[]{:S(2)}) async-start(), calls=%async_computation.2 | async-start | bytes 6881280 | tf_op jit(solution)/shard_map/reduce_scatter | solution.py:131
  377.7 0.7 copy-start.13
Sparse Core Ops, SparseCore 0:
  9.8 269.0 all-gather.2
  370.4 657.1 all-reduce.2
  1031.0 104.0 reduce-scatter.2
